TPU v7x, 256 devices: a whole 4x4x8 slice. The times are simulated.
256 devices in a mesh: dp: 8 (over x, core), seq: 32 (over z, y).
Axes of the slice: x: 4, y: 4, z: 8, core: 2. Of those that a mesh axis runs over, the one named last changes fastest.
Arguments:
- layer_input: bfloat16 [8, 4096, 4096], P('dp', 'seq'), may hold values from -6 to 6
- proj_weight: bfloat16 [4096, 256], replicated, may hold values from -0.0078125 to 0.0078125
- inputs: bfloat16 [8, 4096, 2048], P('dp', 'seq'), may hold values from -6 to 6
- step_size: float32 [8, 32, 4096], P('dp', None, 'seq'), may hold values from 0.02 to 0.2
- log_decay: float32 [8, 32, 4096], P('dp', None, 'seq'), may hold values from -0.8 to 0, as said below
- skip_gain: float32 [32], replicated, may hold values from 0.1 to 1.9
- grad_out: bfloat16 [8, 4096, 2048], P('dp', 'seq'), may hold values from -6 to 6
Outputs:
- grad_inputs: bfloat16 [8, 4096, 2048], P('dp', 'seq')
- grad_weight: float32 [4096, 256], P(('dp', 'seq'))
Inputs may be any that keep to these rules, and one draw needn't show every extreme that they name: `log_decay`: every entry is negative.
All inputs are finite; a program needn't handle non-finite values.
Results may differ from a plain program's by a relative error of at most 0.0069.
Values sent between devices are 32-bit elements; how exact they have to be, the bound alone decides.
A program may use at most 192 MiB of HBM per device.

v0:
```python
import jax
import jax.numpy as jnp
from jax import lax
from jax.sharding import PartitionSpec as P

SHARD_CHANNELS = 32
HEAD_DIM = 64
STATE = 128
SPAN = 128


def span_inputs(proj, inputs, grad_out, step_size, log_decay):
    length = inputs.shape[0]
    spans = length // SPAN
    b_cols = proj[:, :STATE].reshape(spans, SPAN, STATE)
    c_cols = proj[:, STATE:].reshape(spans, SPAN, STATE)
    inputs_c = inputs.reshape(spans, SPAN, SHARD_CHANNELS, HEAD_DIM)
    grad_rows = grad_out.reshape(spans, SPAN, SHARD_CHANNELS, HEAD_DIM)
    step_rows = step_size.reshape(SHARD_CHANNELS, spans, SPAN).transpose(1, 0, 2)
    decay_sum = jnp.cumsum(
        log_decay.reshape(SHARD_CHANNELS, spans, SPAN).transpose(1, 0, 2), axis=2
    )
    span_total = decay_sum[:, :, -1]
    to_end = jnp.exp(span_total[:, :, None] - decay_sum)
    weighted = (
        inputs_c.astype(jnp.float32) * jnp.transpose(step_rows * to_end, (0, 2, 1))[..., None]
    ).astype(jnp.bfloat16)
    scaled = (
        grad_rows.astype(jnp.float32) * jnp.transpose(jnp.exp(decay_sum), (0, 2, 1))[..., None]
    ).astype(jnp.bfloat16)
    own_state = jnp.einsum("cqhp,cqn->chpn", weighted, b_cols, preferred_element_type=jnp.float32)
    own_grad = jnp.einsum("cqhp,cqn->chpn", scaled, c_cols, preferred_element_type=jnp.float32)
    return (
        b_cols,
        c_cols,
        inputs_c,
        grad_rows,
        step_rows,
        decay_sum,
        span_total,
        weighted,
        scaled,
        own_state,
        own_grad,
    )


def span_grads(
    b_cols,
    c_cols,
    inputs_c,
    grad_rows,
    step_rows,
    decay_sum,
    span_total,
    weighted,
    scaled,
    start,
    after,
    skip_gain,
):
    start_bf = start.astype(jnp.bfloat16)
    after_bf = after.astype(jnp.bfloat16)
    row_ids = lax.broadcasted_iota(jnp.int32, (SPAN, SPAN), 0)
    col_ids = lax.broadcasted_iota(jnp.int32, (SPAN, SPAN), 1)
    causal = row_ids >= col_ids
    log_gap = decay_sum[:, :, None] - decay_sum[:, None, :]
    decay_mat = jnp.exp(jnp.where(causal[None], log_gap, -jnp.inf))
    kernel = jnp.dot(c_cols, b_cols.T, preferred_element_type=jnp.float32)
    weights = (decay_mat * kernel[None]).astype(jnp.bfloat16)
    within = jnp.einsum("hsj,shp->jhp", weights, grad_rows, preferred_element_type=jnp.float32)
    carried = jnp.einsum("hpn,jn->jhp", after_bf, b_cols, preferred_element_type=jnp.float32)
    to_end = jnp.exp(span_total[:, None] - decay_sum)
    grad_x = step_rows.T[:, :, None] * (within + to_end.T[:, :, None] * carried) + skip_gain[
        None, :, None
    ] * grad_rows.astype(jnp.float32)
    intersection = jnp.einsum(
        "shp,jhp->hsj", grad_rows, inputs_c, preferred_element_type=jnp.float32
    )
    mixing = jnp.sum(decay_mat * step_rows[:, None, :] * intersection, axis=0).astype(jnp.bfloat16)
    grad_c = jnp.dot(mixing, b_cols, preferred_element_type=jnp.float32) + jnp.dot(
        scaled.reshape(SPAN, -1), start_bf.reshape(-1, STATE), preferred_element_type=jnp.float32
    )
    grad_b = jnp.dot(mixing.T, c_cols, preferred_element_type=jnp.float32) + jnp.dot(
        weighted.reshape(SPAN, -1), after_bf.reshape(-1, STATE), preferred_element_type=jnp.float32
    )
    grad_proj = jnp.concatenate([grad_b, grad_c], axis=1).astype(jnp.bfloat16)
    return (grad_x.astype(jnp.bfloat16).reshape(SPAN, -1), grad_proj)


def exchange(own_state, own_grad, device_total):
    count = lax.axis_size("seq")
    heads, rows, cols = own_state.shape
    marks = jnp.broadcast_to(device_total[:, None, None], (heads, 8, cols))
    payload = jnp.stack(
        [jnp.concatenate([own_state, marks], axis=1), jnp.concatenate([own_grad, marks], axis=1)]
    )
    mine = lax.all_to_all(payload, "seq", 1, 1, tiled=True)
    totals = mine[0, :, rows, 0]
    ends = mine[:, :, :rows, :].reshape(2, count, rows * cols)
    ids = jnp.arange(count)
    target, source, between = (ids[:, None, None], ids[None, :, None], ids[None, None, :])
    fwd_span = (source < between) & (between < target)
    bwd_span = (target < between) & (between < source)
    fwd_log = jnp.sum(jnp.where(fwd_span, totals[None, None, :], 0.0), axis=2)
    bwd_log = jnp.sum(jnp.where(bwd_span, totals[None, None, :], 0.0), axis=2)
    fwd_w = jnp.where(ids[None, :] < ids[:, None], jnp.exp(fwd_log), 0.0)
    bwd_w = jnp.where(ids[None, :] > ids[:, None], jnp.exp(bwd_log), 0.0)
    weights = jnp.stack([fwd_w, bwd_w])
    entries = jnp.einsum(
        "ktj,kjx->ktx",
        weights,
        ends,
        precision=lax.Precision.HIGHEST,
        preferred_element_type=jnp.float32,
    ).reshape(2, count, rows, cols)
    back = lax.all_to_all(entries, "seq", 1, 1, tiled=True)
    return (back[0], back[1])


def scatter_rows(term):
    dp, seq = (lax.axis_size("dp"), lax.axis_size("seq"))
    rows, cols = term.shape
    part = lax.all_to_all(term.reshape(dp, rows // dp, cols), "dp", 0, 0, tiled=True).sum(0)
    part = lax.all_to_all(part.reshape(seq, rows // dp // seq, cols), "seq", 0, 0, tiled=True)
    return part.sum(0)


def on_device(layer_input, proj_weight, inputs, step_size, log_decay, skip_gain, grad_out):
    tokens = layer_input[0]
    length = tokens.shape[0]
    proj = jnp.dot(tokens, proj_weight, preferred_element_type=jnp.float32).astype(jnp.bfloat16)
    pieces = span_inputs(proj, inputs[0], grad_out[0], step_size[0], log_decay[0])
    own_state, own_grad, span_total = (pieces[9], pieces[10], pieces[6])
    empty_state = jnp.zeros((SHARD_CHANNELS, HEAD_DIM, STATE), jnp.float32)

    def advance(state_carry, piece):
        return (jnp.exp(piece[1])[:, None, None] * state_carry + piece[0], state_carry)

    last_state, local_starts = lax.scan(advance, empty_state, (own_state, span_total))
    last_grad, local_afters = lax.scan(advance, empty_state, (own_grad, span_total), reverse=True)
    state_entry, grad_entry = exchange(last_state, last_grad, jnp.sum(span_total, axis=0))
    running = jnp.cumsum(span_total, axis=0)
    before = running - span_total
    behind = jnp.sum(span_total, axis=0)[None] - running
    starts = local_starts + jnp.exp(before)[:, :, None, None] * state_entry[None]
    afters = local_afters + jnp.exp(behind)[:, :, None, None] * grad_entry[None]

    def finish(parts):
        return span_grads(*parts, skip_gain)

    grad_x, grad_proj = lax.map(finish, pieces[:9] + (starts, afters))
    grad_proj = grad_proj.reshape(length, 2 * STATE)
    scale_factor = 1.0 / (length * lax.axis_size("seq"))
    term = jnp.einsum("ld,ln->dn", tokens, grad_proj, preferred_element_type=jnp.float32)
    grad_weight = scatter_rows(term) * scale_factor
    return (grad_x, grad_weight)


def solution(mesh):
    return jax.shard_map(
        on_device,
        mesh=mesh,
        in_specs=(
            P("dp", "seq", None),
            P(),
            P("dp", "seq", None),
            P("dp", None, "seq"),
            P("dp", None, "seq"),
            P(),
            P("dp", "seq", None),
        ),
        out_specs=(P("dp", "seq", None), P(("dp", "seq"), None)),
        check_vma=False,
    )
```

profile of v0, /device:TPU:32, one launch (start us, length us, event | category | flops | bytes accessed | tf_op | source)
XLA Modules:
  0.0 235.9 jit_solution(15632578017909510652)
XLA Ops:
  0.6 0.0 copy-start
  0.6 1.1 reduce_window_sum.17
  1.8 0.2 slice_reduce_fusion.1
  2.0 0.8 multiply_bitcast_fusion
  2.8 1.3 copy.43
  4.1 1.3 copy.42
  5.4 0.0 copy-done
  5.4 1.7 convolution_convert_fusion
  7.1 0.2 fusion.13
  7.3 0.3 convolution_add_fusion.1
  7.6 0.3 convolution_add_fusion
  7.9 0.1 broadcast_in_dim.100
  8.0 0.2 fusion.6
  8.2 0.2 pad_maximum_fusion
  8.4 1.6 copy.45
  9.9 11.4 %all-to-all-start = ((f32[2,32,72,128]{3,2,0,1:T(8,128)}), f32[2,32,72,128]{3,2,0,1:T(8,128)}, u32[]{:S(2)}, u32[]{:S(2)}) async-start(f32[2,32,72,128]{3,2,0,1:T(8,128)} %copy.45), calls=%async_computation | async-start | bytes 4718592 | tf_op jit(solution)/shard_map/all_to_all | solution.py:98
  21.4 55.3 %all-to-all-done = f32[2,32,72,128]{3,2,0,1:T(8,128)} async-done(((f32[2,32,72,128]{3,2,0,1:T(8,128)}), f32[2,32,72,128]{3,2,0,1:T(8,128)}, u32[]{:S(2)}, u32[]{:S(2)}) %all-to-all-start) | async-done | bytes 2359328 | tf_op jit(solution)/shard_map/all_to_all | solution.py:98
  76.7 3.2 %slice.32 = f32[2,32,64,128]{3,2,0,1:T(8,128)} slice(f32[2,32,72,128]{3,2,0,1:T(8,128)} %all-to-all-done), slice={[0:2], [0:32], [0:64], [0:128]} | slice | bytes 4194304 | tf_op jit(solution)/shard_map/slice | solution.py:100
  79.9 3.4 %reshape.335 = f32[2,32,8192]{2,0,1:T(2,128)} reshape(f32[2,32,64,128]{3,2,0,1:T(8,128)} %slice.32) | data formatting | bytes 4194304 | tf_op jit(solution)/shard_map/reshape | solution.py:100
  83.3 1.2 slice_reduce_fusion
  84.5 0.3 select_reduce_fusion.1
  84.9 4.5 %fusion = f32[2,32,8192]{2,1,0:T(8,128)S(1)} fusion(f32[2,32,8192]{2,0,1:T(2,128)} %reshape.335, f32[1,32,32]{2,1,0:T(8,128)S(1)} %bitcast_select_fusion, f32[1,32,32]{2,1,0:T(8,128)S(1)} %bitcast_select_fusion.1), kind=kOutput, calls=%fused_computation.2 | convolution fusion | flops 201328640 | bytes 4202496 | tf_op jit(solution)/shard_map/ktj,kjx->ktx/dot_general | solution.py:110
  89.4 0.4 copy.56
  89.8 1.4 copy.47
  91.3 0.0 copy-start.4
  91.3 6.6 %all-to-all-start.1 = ((f32[2,32,64,128]{3,2,0,1:T(8,128)}), f32[2,32,64,128]{3,2,0,1:T(8,128)}, u32[]{:S(2)}, u32[]{:S(2)}) async-start(f32[2,32,64,128]{3,2,0,1:T(8,128)} %copy.47), calls=%async_computation.1 | async-start | bytes 4194304 | tf_op jit(solution)/shard_map/all_to_all | solution.py:117
  97.9 0.0 copy-done.4
  97.9 1.1 multiply_reduce_fusion
  99.1 0.2 fusion.39
  99.3 0.2 fusion.33
  99.5 1.3 fusion.10
  100.8 45.9 %all-to-all-done.1 = f32[2,32,64,128]{3,2,0,1:T(8,128)} async-done(((f32[2,32,64,128]{3,2,0,1:T(8,128)}), f32[2,32,64,128]{3,2,0,1:T(8,128)}, u32[]{:S(2)}, u32[]{:S(2)}) %all-to-all-start.1) | async-done | bytes 2097184 | tf_op jit(solution)/shard_map/all_to_all | solution.py:117
  146.7 0.0 copy-start.3
  146.7 0.0 copy-start.2
  146.7 0.0 copy-start.1
  146.7 1.9 fusion.11
  148.6 0.0 copy-done.3
  148.6 0.3 fusion.9
  149.0 0.0 copy-done.2
  149.0 0.4 fusion.8
  149.4 0.0 copy-done.1
  149.4 0.7 fusion.15
  150.1 0.6 copy.60
  150.7 54.5 %all_to_all.20 = f32[8,512,256]{1,2,0:T(8,128)} all-to-all(f32[8,512,256]{1,2,0:T(8,128)S(1)} %bitcast.93), channel_id=1, replica_groups=mesh['dp'=8,'seq'=32] {'dp'}, dimensions={0} | all-to-all | bytes 8388608 | tf_op jit(solution)/shard_map/all_to_all | solution.py:124
  205.2 3.5 %reduce_sum.57 = f32[512,256]{0,1:T(8,128)} reduce(f32[8,512,256]{1,2,0:T(8,128)} %all_to_all.20, f32[]{:T(128)} %constant.57.clone.1), dimensions={0}, to_apply=%region_4.5 | reduce | flops 917504 | bytes 4718596 | tf_op jit(solution)/shard_map/reduce_sum | solution.py:124
  208.7 0.0 copy-start.5
  208.7 2.1 copy.51
  210.8 6.5 %all-to-all-start.3 = ((f32[32,16,256]{2,1,0:T(8,128)}), f32[32,16,256]{2,1,0:T(8,128)}, u32[]{:S(2)}, u32[]{:S(2)}) async-start(f32[32,16,256]{2,1,0:T(8,128)} %bitcast.102), calls=%async_computation.3 | async-start | bytes 1048576 | tf_op jit(solution)/shard_map/all_to_all | solution.py:125
  217.3 0.1 exponential_bitcast_fusion.1
  217.4 0.1 fusion.36
  217.5 0.3 convolution_multiply_fusion
  217.8 0.0 copy-done.5
  217.8 1.2 fusion.5
  219.0 1.0 copy.52
  220.0 14.2 %all-to-all-done.3 = f32[32,16,256]{2,1,0:T(8,128)} async-done(((f32[32,16,256]{2,1,0:T(8,128)}), f32[32,16,256]{2,1,0:T(8,128)}, u32[]{:S(2)}, u32[]{:S(2)}) %all-to-all-start.3) | async-done | bytes 524320 | tf_op jit(solution)/shard_map/all_to_all | solution.py:125
  234.2 1.1 reduce_sum.58
  235.3 0.6 broadcast_multiply_fusion
  (5 shorter events, 0.1 us)
Async XLA Ops:
  0.6 4.8 %copy-start = (bf16[4096,256]{1,0:T(8,128)(2,1)S(1)}, bf16[4096,256]{1,0:T(8,128)(2,1)}, u32[]{:S(2)}) copy-start(bf16[4096,256]{1,0:T(8,128)(2,1)} %param.8) | copy-start | bytes 6291460
  9.9 66.7 %all-to-all-start = ((f32[2,32,72,128]{3,2,0,1:T(8,128)}), f32[2,32,72,128]{3,2,0,1:T(8,128)}, u32[]{:S(2)}, u32[]{:S(2)}) async-start(f32[2,32,72,128]{3,2,0,1:T(8,128)} %copy.45), calls=%async_computation | async-start | bytes 4718592 | tf_op jit(solution)/shard_map/all_to_all | solution.py:98
  91.3 6.7 %copy-start.4 = (f32[1,32,128]{2,1,0:T(8,128)S(1)}, f32[1,32,128]{2,1,0:T(8,128)}, u32[]{:S(2)}) copy-start(f32[1,32,128]{2,1,0:T(8,128)} %param.10) | copy-start | bytes 49156
  91.3 55.4 %all-to-all-start.1 = ((f32[2,32,64,128]{3,2,0,1:T(8,128)}), f32[2,32,64,128]{3,2,0,1:T(8,128)}, u32[]{:S(2)}, u32[]{:S(2)}) async-start(f32[2,32,64,128]{3,2,0,1:T(8,128)} %copy.47), calls=%async_computation.1 | async-start | bytes 4194304 | tf_op jit(solution)/shard_map/all_to_all | solution.py:117
  146.7 1.9 copy-start.3
  146.7 2.3 copy-start.2
  146.7 2.7 %copy-start.1 = (bf16[1,128,4096]{2,1,0:T(8,128)(2,1)S(1)}, bf16[1,128,4096]{2,1,0:T(8,128)(2,1)}, u32[]{:S(2)}) copy-start(bf16[1,128,4096]{2,1,0:T(8,128)(2,1)} %param.7) | copy-start | bytes 3145732
  208.7 9.1 %copy-start.5 = (f32[32]{0:T(128)S(1)}, f32[32]{0:T(128)}, u32[]{:S(2)}) copy-start(f32[32]{0:T(128)} %param.12) | copy-start | bytes 388
  210.8 23.4 %all-to-all-start.3 = ((f32[32,16,256]{2,1,0:T(8,128)}), f32[32,16,256]{2,1,0:T(8,128)}, u32[]{:S(2)}, u32[]{:S(2)}) async-start(f32[32,16,256]{2,1,0:T(8,128)} %bitcast.102), calls=%async_computation.3 | async-start | bytes 1048576 | tf_op jit(solution)/shard_map/all_to_all | solution.py:125
where the time goes:
time: 237 us; the launch traced here: 236 us
  waiting for transfers between devices  115 us (49%)
  blocking collectives  54.5 us (23%)
  starting transfers between devices  24.6 us (10%)
  local copies, waits for them, and re-layouts  17.8 us (8%)
  other arithmetic  11.4 us (5%)
  matrix products  11.3 us (5%)
    all_to_all x1, waiting for transfers between devices, exchange(): mine = lax.all_to_all(payload, 'seq', 1, 1, tiled=True)  55.3 us
    all_to_all x1, blocking collectives, scatter_rows(): lax.all_to_all(term.reshape(dp, rows // dp, cols), 'dp', 0, 0, tiled=True)  54.5 us
    all_to_all x1, waiting for transfers between devices, exchange(): back = lax.all_to_all(entries, 'seq', 1, 1, tiled=True)  45.9 us
    all_to_all x1, waiting for transfers between devices, scatter_rows(): lax.all_to_all(part.reshape(seq, rows // dp // seq, cols), 'seq', 0, 0, t...  14.2 us
    all_to_all x1, starting transfers between devices, exchange(): mine = lax.all_to_all(payload, 'seq', 1, 1, tiled=True)  11.4 us
    all_to_all x1, starting transfers between devices, exchange(): back = lax.all_to_all(entries, 'seq', 1, 1, tiled=True)  6.64 us
    all_to_all x1, starting transfers between devices, scatter_rows(): lax.all_to_all(part.reshape(seq, rows // dp // seq, cols), 'seq', 0, 0, t...  6.52 us
  transfers between devices with their start and end apart: 3, of which 3 were waited for; matrix products, arithmetic and copies ran while one was open for 2% of the time, Pallas kernels for 0%

commit v1 on v0

--- a/solution.py
+++ b/solution.py
@@ -114,7 +114,10 @@
         precision=lax.Precision.HIGHEST,
         preferred_element_type=jnp.float32,
     ).reshape(2, count, rows, cols)
-    back = lax.all_to_all(entries, "seq", 1, 1, tiled=True)
+    back = jnp.concatenate(
+        lax.all_to_all(jnp.stack(jnp.split(entries, lax.axis_size("seq"), axis=1)), "seq", 0, 0),
+        axis=1,
+    )
     return (back[0], back[1])
 
 

time: 237 us -> 252 us (1.063)
  local copies, waits for them, and re-layouts: 17.8 us -> 36.3 us
  waiting for transfers between devices: 115 us -> 112 us
    unnamed x16 -> x47, local copies, waits for them, and re-layouts: 4.04 us -> 24.4 us
    all_to_all x1, waiting for transfers between devices: 14.2 us -> 11.1 us  [scatter_rows(): lax.all_to_all(part.reshape(seq, rows // dp // seq, cols), 'seq', 0, 0, t...]
  transfers between devices with their start and end apart: 3 -> 3, of which waited for: 3 -> 3; matrix products, arithmetic and copies ran while one was open for 2% -> 3% of each run, Pallas kernels for 0% -> 0%
where the time goes in v1:
time: 252 us; the launch traced here: 251 us
  waiting for transfers between devices  112 us (44%)
  blocking collectives  54.5 us (22%)
  local copies, waits for them, and re-layouts  36.3 us (14%)
  starting transfers between devices  24.5 us (10%)
  matrix products  13.3 us (5%)
  other arithmetic  9.55 us (4%)
    all_to_all x1, waiting for transfers between devices, exchange(): mine = lax.all_to_all(payload, 'seq', 1, 1, tiled=True)  55.3 us
    all_to_all x1, blocking collectives, scatter_rows(): lax.all_to_all(term.reshape(dp, rows // dp, cols), 'dp', 0, 0, tiled=True)  54.5 us
    all_to_all x1, waiting for transfers between devices, exchange(): lax.all_to_all(jnp.stack(jnp.split(entries, lax.axis_size('seq'), axis=1)...  45.9 us
    unnamed x47, local copies, waits for them, and re-layouts  24.4 us
    all_to_all x1, starting transfers between devices, exchange(): mine = lax.all_to_all(payload, 'seq', 1, 1, tiled=True)  11.4 us
    all_to_all x1, waiting for transfers between devices, scatter_rows(): lax.all_to_all(part.reshape(seq, rows // dp // seq, cols), 'seq', 0, 0, t...  11.1 us
    all_to_all x1, starting transfers between devices, exchange(): lax.all_to_all(jnp.stack(jnp.split(entries, lax.axis_size('seq'), axis=1)...  6.64 us
    all_to_all x1, starting transfers between devices, scatter_rows(): lax.all_to_all(part.reshape(seq, rows // dp // seq, cols), 'seq', 0, 0, t...  6.46 us
  transfers between devices with their start and end apart: 3, of which 3 were waited for; matrix products, arithmetic and copies ran while one was open for 3% of the time, Pallas kernels for 0%

profile of v1, /device:TPU:32, one launch (start us, length us, event | category | flops | bytes accessed | tf_op | source)
XLA Modules:
  0.0 251.4 jit_solution(4525466821424008442)
XLA Ops:
  0.6 1.1 reduce_window_sum.17
  2.0 0.8 multiply_bitcast_fusion
  2.8 1.3 copy.169
  4.1 1.3 copy.168
  5.4 1.7 convolution_convert_fusion
  8.4 1.6 copy.171
  9.9 11.4 %all-to-all-start = ((f32[2,32,72,128]{3,2,0,1:T(8,128)}), f32[2,32,72,128]{3,2,0,1:T(8,128)}, u32[]{:S(2)}, u32[]{:S(2)}) async-start(f32[2,32,72,128]{3,2,0,1:T(8,128)} %copy.171), calls=%async_computation | async-start | bytes 4718592 | tf_op jit(solution)/shard_map/all_to_all | solution.py:98
  21.4 55.3 %all-to-all-done = f32[2,32,72,128]{3,2,0,1:T(8,128)} async-done(((f32[2,32,72,128]{3,2,0,1:T(8,128)}), f32[2,32,72,128]{3,2,0,1:T(8,128)}, u32[]{:S(2)}, u32[]{:S(2)}) %all-to-all-start) | async-done | bytes 2359328 | tf_op jit(solution)/shard_map/all_to_all | solution.py:98
  76.7 3.2 %slice.37 = f32[2,32,64,128]{3,2,0,1:T(8,128)} slice(f32[2,32,72,128]{3,2,0,1:T(8,128)} %all-to-all-done), slice={[0:2], [0:32], [0:64], [0:128]} | slice | bytes 4194304 | tf_op jit(solution)/shard_map/slice | solution.py:100
  79.9 3.4 %reshape.361 = f32[2,32,8192]{2,0,1:T(2,128)} reshape(f32[2,32,64,128]{3,2,0,1:T(8,128)} %slice.37) | data formatting | bytes 4194304 | tf_op jit(solution)/shard_map/reshape | solution.py:100
  83.3 1.2 slice_reduce_fusion
  84.5 0.3 select_reduce_fusion.1
  84.9 4.5 %fusion = f32[2,32,8192]{2,1,0:T(8,128)S(1)} fusion(f32[2,32,8192]{2,0,1:T(2,128)} %reshape.361, f32[1,32,32]{2,1,0:T(8,128)S(1)} %bitcast_select_fusion, f32[1,32,32]{2,1,0:T(8,128)S(1)} %bitcast_select_fusion.1), kind=kOutput, calls=%fused_computation.2 | convolution fusion | flops 201328640 | bytes 4202496 | tf_op jit(solution)/shard_map/ktj,kjx->ktx/dot_general | solution.py:110
  89.4 0.4 copy.245
  89.8 0.6 constant_dynamic-update-slice_fusion.31
  90.5 0.6 constant_dynamic-update-slice_fusion.30
  91.1 0.6 constant_dynamic-update-slice_fusion.29
  91.7 0.6 constant_dynamic-update-slice_fusion.28
  92.3 0.6 constant_dynamic-update-slice_fusion.27
  92.9 0.6 constant_dynamic-update-slice_fusion.26
  93.6 0.6 constant_dynamic-update-slice_fusion.25
  94.2 0.6 constant_dynamic-update-slice_fusion.24
  94.8 0.6 constant_dynamic-update-slice_fusion.23
  95.4 0.6 constant_dynamic-update-slice_fusion.22
  96.1 0.6 constant_dynamic-update-slice_fusion.21
  96.7 0.6 constant_dynamic-update-slice_fusion.20
  97.3 0.6 constant_dynamic-update-slice_fusion.19
  97.9 0.6 constant_dynamic-update-slice_fusion.18
  98.6 0.6 constant_dynamic-update-slice_fusion.17
  99.2 0.6 constant_dynamic-update-slice_fusion.16
  99.8 0.6 constant_dynamic-update-slice_fusion.15
  100.4 0.6 constant_dynamic-update-slice_fusion.14
  101.1 0.6 constant_dynamic-update-slice_fusion.13
  101.7 0.6 constant_dynamic-update-slice_fusion.12
  102.3 0.6 constant_dynamic-update-slice_fusion.11
  102.9 0.6 constant_dynamic-update-slice_fusion.10
  103.5 0.6 constant_dynamic-update-slice_fusion.9
  104.2 0.6 constant_dynamic-update-slice_fusion.8
  104.8 0.6 constant_dynamic-update-slice_fusion.7
  105.4 0.6 constant_dynamic-update-slice_fusion.6
  106.0 0.6 constant_dynamic-update-slice_fusion.5
  106.7 0.6 constant_dynamic-update-slice_fusion.4
  107.3 0.6 constant_dynamic-update-slice_fusion.3
  107.9 0.6 constant_dynamic-update-slice_fusion.2
  108.5 0.6 constant_dynamic-update-slice_fusion.1
  109.1 0.6 constant_dynamic-update-slice_fusion
  109.8 6.6 %all-to-all-start.1 = ((f32[32,2,1,64,128]{4,3,2,1,0:T(8,128)}), f32[32,2,1,64,128]{4,3,2,1,0:T(8,128)}, u32[]{:S(2)}, u32[]{:S(2)}) async-start(f32[32,2,1,64,128]{4,3,2,1,0:T(8,128)} %constant_dynamic-update-slice_fusion), calls=%async_computation.1 | async-start | bytes 4194304 | tf_op jit(solution)/shard_map/all_to_all | solution.py:118
  116.5 1.1 multiply_reduce_fusion
  118.0 1.3 fusion.10
  119.3 45.9 %all-to-all-done.1 = f32[32,2,1,64,128]{4,3,2,1,0:T(8,128)} async-done(((f32[32,2,1,64,128]{4,3,2,1,0:T(8,128)}), f32[32,2,1,64,128]{4,3,2,1,0:T(8,128)}, u32[]{:S(2)}, u32[]{:S(2)}) %all-to-all-start.1) | async-done | bytes 2097184 | tf_op jit(solution)/shard_map/all_to_all | solution.py:118
  165.2 1.9 multiply_convert_fusion.2
  167.1 0.4 fusion.8
  167.5 0.4 fusion.9
  167.9 0.7 fusion.15
  168.6 0.6 copy.249
  169.2 54.5 %all_to_all.20 = f32[8,512,256]{1,2,0:T(8,128)} all-to-all(f32[8,512,256]{1,2,0:T(8,128)S(1)} %bitcast.288), channel_id=1, replica_groups=mesh['dp'=8,'seq'=32] {'dp'}, dimensions={0} | all-to-all | bytes 8388608 | tf_op jit(solution)/shard_map/all_to_all | solution.py:127
  223.7 2.7 %reduce_sum.57 = f32[512,256]{0,1:T(8,128)S(1)} reduce(f32[8,512,256]{1,2,0:T(8,128)} %all_to_all.20, f32[]{:T(128)} %constant.57.clone.1), dimensions={0}, to_apply=%region_4.5 | reduce | flops 917504 | bytes 4718596 | tf_op jit(solution)/shard_map/reduce_sum | solution.py:127
  226.4 1.0 copy.208
  227.4 6.5 %all-to-all-start.3 = ((f32[32,16,256]{2,1,0:T(8,128)}), f32[32,16,256]{2,1,0:T(8,128)S(1)}, u32[]{:S(2)}, u32[]{:S(2)}) async-start(f32[32,16,256]{2,1,0:T(8,128)} %bitcast.327), calls=%async_computation.3 | async-start | bytes 1048576 | tf_op jit(solution)/shard_map/all_to_all | solution.py:128
  234.1 1.6 convolution_multiply_fusion
  235.7 1.9 fusion.5
  237.6 2.0 copy.209
  239.6 11.1 %all-to-all-done.3 = f32[32,16,256]{2,1,0:T(8,128)S(1)} async-done(((f32[32,16,256]{2,1,0:T(8,128)}), f32[32,16,256]{2,1,0:T(8,128)S(1)}, u32[]{:S(2)}, u32[]{:S(2)}) %all-to-all-start.3) | async-done | bytes 524320 | tf_op jit(solution)/shard_map/all_to_all | solution.py:128
  250.8 0.6 broadcast_multiply_fusion
  (29 shorter events, 2.1 us)
Async XLA Ops:
  0.6 4.8 %copy-start = (bf16[4096,256]{1,0:T(8,128)(2,1)S(1)}, bf16[4096,256]{1,0:T(8,128)(2,1)}, u32[]{:S(2)}) copy-start(bf16[4096,256]{1,0:T(8,128)(2,1)} %param.8) | copy-start | bytes 6291460
  9.9 66.7 %all-to-all-start = ((f32[2,32,72,128]{3,2,0,1:T(8,128)}), f32[2,32,72,128]{3,2,0,1:T(8,128)}, u32[]{:S(2)}, u32[]{:S(2)}) async-start(f32[2,32,72,128]{3,2,0,1:T(8,128)} %copy.171), calls=%async_computation | async-start | bytes 4718592 | tf_op jit(solution)/shard_map/all_to_all | solution.py:98
  109.8 6.7 %copy-start.4 = (f32[1,32,128]{2,1,0:T(8,128)S(1)}, f32[1,32,128]{2,1,0:T(8,128)}, u32[]{:S(2)}) copy-start(f32[1,32,128]{2,1,0:T(8,128)} %param.10) | copy-start | bytes 49156
  109.8 55.4 %all-to-all-start.1 = ((f32[32,2,1,64,128]{4,3,2,1,0:T(8,128)}), f32[32,2,1,64,128]{4,3,2,1,0:T(8,128)}, u32[]{:S(2)}, u32[]{:S(2)}) async-start(f32[32,2,1,64,128]{4,3,2,1,0:T(8,128)} %constant_dynamic-update-slice_fusion), calls=%async_computation.1 | async-start | bytes 4194304 | tf_op jit(solution)/shard_map/all_to_all | solution.py:118
  119.3 47.8 %copy-start.3 = (bf16[128,32,64]{0,2,1:T(8,128)(2,1)S(1)}, bf16[128,32,64]{0,2,1:T(8,128)(2,1)}, u32[]{:S(2)}) copy-start(bf16[128,32,64]{0,2,1:T(8,128)(2,1)} %get-tuple-element.83) | copy-start | bytes 1572868
  165.2 2.3 copy-start.2
  165.2 2.6 %copy-start.1 = (bf16[1,128,4096]{2,1,0:T(8,128)(2,1)S(1)}, bf16[1,128,4096]{2,1,0:T(8,128)(2,1)}, u32[]{:S(2)}) copy-start(bf16[1,128,4096]{2,1,0:T(8,128)(2,1)} %param.7) | copy-start | bytes 3145732
  226.4 9.3 %copy-start.5 = (f32[32]{0:T(128)S(1)}, f32[32]{0:T(128)}, u32[]{:S(2)}) copy-start(f32[32]{0:T(128)} %param.12) | copy-start | bytes 388
  227.4 23.3 %all-to-all-start.3 = ((f32[32,16,256]{2,1,0:T(8,128)}), f32[32,16,256]{2,1,0:T(8,128)S(1)}, u32[]{:S(2)}, u32[]{:S(2)}) async-start(f32[32,16,256]{2,1,0:T(8,128)} %bitcast.327), calls=%async_computation.3 | async-start | bytes 1048576 | tf_op jit(solution)/shard_map/all_to_all | solution.py:128
